TPU v7x, 128 devices: a whole 4x4x4 slice. The times are simulated.
128 devices in a mesh: row: 32 (over x, z, core), col: 4 (over y).
Axes of the slice: x: 4, y: 4, z: 4, core: 2. Of those that a mesh axis runs over, the one named last changes fastest.
Arguments:
- front: float32 [3, 32, 24, 4, 128, 128], P(None, 'row', None, 'col'), may hold values from -6 to 6
- child_tiles: float32 [8192, 128, 128], P(('row', 'col')), may hold values from -6 to 6
- tile_dest: int32 [8192, 1], P(('row', 'col')), may hold values from 0 to 127; in each aligned block of 64 rows (0 to 63, 64 to 127, ...) no two rows name the same one
- tile_slot: int32 [8192], P(('row', 'col')), may hold values from 0 to 71
- tile_count: int32 [128], P(('row', 'col')), may hold values from 48 to 64, as said below
- diag_inverses: float32 [2, 256, 256], replicated, as said below
Outputs:
- factored: float32 [3, 32, 24, 4, 128, 128], P(None, 'row', None, 'col')
Inputs may be any that keep to these rules, and one draw needn't show every extreme that they name: Among the 64 slots of one device, no two name the same device in tile_dest, live or not; every device is named by some slot. `tile_count`: some device has all 64 slots live. `diag_inverses`: each matrix is upper triangular with a positive diagonal; it is given as it is and need not match any diagonal block of the front.
All inputs are finite; a program needn't handle non-finite values.
Results may differ from a plain program's by a relative error of at most 0.000068.
Values sent between devices are 32-bit elements; how exact they have to be, the bound alone decides.
A program may use at most 128 MiB of HBM per device.

v0:
```python
import jax
import jax.numpy as jnp
from jax import lax
from jax.sharding import PartitionSpec as P


def panel_part(field, inverse, first, my_col, n_col):
    rows_here, tile = (field.shape[0], field.shape[2])
    total = jnp.zeros((rows_here * tile, 2 * tile), jnp.float32)
    for offset in range(2):
        target = first + offset
        local_b = target // n_col
        owner = target % n_col
        column = field[:, local_b].reshape(rows_here * tile, tile)
        term = jnp.dot(
            column, inverse[offset * tile : (offset + 1) * tile], precision=lax.Precision.HIGHEST
        )
        total = total + jnp.where(my_col == owner, term, jnp.zeros_like(term))
    return total


def panel_rows(field, inverse, first, my_row, my_col, n_row, n_col):
    rows_here, tile = (field.shape[0], field.shape[2])
    total = panel_part(field, inverse, first, my_col, n_col).reshape(rows_here, tile, 2 * tile)
    tile_row = jnp.arange(rows_here, dtype=jnp.int32) * n_row + my_row
    total = jnp.where((tile_row >= first)[:, None, None], total, jnp.zeros_like(total))
    summed = lax.psum(total, "col")
    return summed


def column_side(rows_three, cols_here, my_col, n_col):
    rows_here, tile = (rows_three.shape[0], rows_three.shape[1])
    whole = lax.all_gather(
        rows_three.reshape(rows_here, 1, tile, 2 * tile), "row", axis=1, tiled=True
    )
    ordered = whole.reshape(cols_here, n_col, tile, 2 * tile)
    return lax.dynamic_index_in_dim(ordered, my_col, axis=1, keepdims=False)


def trailing(field, rows_three, cols_three, limit, my_row, my_col, n_row, n_col):
    rows_here, cols_here = (field.shape[0], field.shape[1])
    tile_row = jnp.arange(rows_here, dtype=jnp.int32) * n_row + my_row
    tile_col = jnp.arange(cols_here, dtype=jnp.int32) * n_col + my_col
    keep = (tile_row >= limit)[:, None] & (tile_col >= limit)[None, :]
    update = jnp.einsum("aik,bjk->abij", rows_three, cols_three, precision=lax.Precision.HIGHEST)
    return field - jnp.where(keep[:, :, None, None], update, jnp.zeros_like(update))


def body(front, child_tiles, tile_dest, tile_slot, tile_count, diag_inverses):
    n_row = lax.axis_size("row")
    n_col = lax.axis_size("col")
    my_row = lax.axis_index("row")
    my_col = lax.axis_index("col")
    rows_here, cols_here, tile = (front.shape[0], front.shape[2], front.shape[4])
    slots = child_tiles.shape[0]
    devices = n_row * n_col
    live = jnp.arange(slots, dtype=jnp.int32) < tile_count[0]
    hits = (tile_dest[:, 0][None, :] == jnp.arange(devices, dtype=jnp.int32)[:, None]) & live[
        None, :
    ]
    found = jnp.any(hits, axis=1)
    picked = jnp.sum(hits.astype(jnp.int32) * jnp.arange(slots, dtype=jnp.int32)[None, :], axis=1)
    outgoing = jnp.take(child_tiles, picked, axis=0)
    outgoing = jnp.where(found[:, None, None], outgoing, jnp.zeros_like(outgoing))
    slot_out = jnp.where(found, jnp.take(tile_slot, picked).astype(jnp.float32), jnp.float32(-1.0))
    incoming, slot_in = (
        lax.all_to_all(outgoing, ("row", "col"), split_axis=0, concat_axis=0, tiled=True),
        lax.all_to_all(slot_out, ("row", "col"), split_axis=0, concat_axis=0, tiled=True),
    )
    placing = (
        slot_in[None, :] == jnp.arange(rows_here * cols_here, dtype=jnp.float32)[:, None]
    ).astype(jnp.float32)
    added = jnp.dot(
        placing, incoming.reshape(devices, tile * tile), precision=lax.Precision.HIGHEST
    )
    field = front[:, 0, :, 0] + added.reshape(rows_here, cols_here, tile, tile)
    rows_one = panel_rows(field, diag_inverses[0], 0, my_row, my_col, n_row, n_col)
    cols_one = column_side(rows_one, cols_here, my_col, n_col)
    field = trailing(field, rows_one, cols_one, 2, my_row, my_col, n_row, n_col)
    rows_two = panel_rows(field, diag_inverses[1], 2, my_row, my_col, n_row, n_col)
    cols_two = column_side(rows_two, cols_here, my_col, n_col)
    field = trailing(field, rows_two, cols_two, 4, my_row, my_col, n_row, n_col)
    for panel_index, rows_three in ((0, rows_one), (1, rows_two)):
        for offset in range(2):
            target = 2 * panel_index + offset
            local_b = target // n_col
            owner = target % n_col
            piece = rows_three[:, :, offset * tile : (offset + 1) * tile]
            field = field.at[:, local_b].set(jnp.where(my_col == owner, piece, field[:, local_b]))
    return field[:, None, :, None]


def solution(mesh):
    return jax.shard_map(
        body,
        mesh=mesh,
        in_specs=(
            P(None, "row", None, "col", None, None),
            P(("row", "col"), None, None),
            P(("row", "col"), None),
            P(("row", "col")),
            P(("row", "col")),
            P(),
        ),
        out_specs=P(None, "row", None, "col", None, None),
        check_vma=False,
    )
```

profile of v0, /device:TPU:1, one launch (start us, length us, event | category | flops | bytes accessed | tf_op | source)
XLA Modules:
  0.0 462.4 jit_solution(310653920112481245)
XLA Ops:
  7.2 0.8 select_reduce_fusion
  8.0 0.8 fusion.27
  8.8 1.2 gather_fusion
  10.0 0.7 copy.46
  10.8 11.5 %all-to-all-start = ((f32[128,1,1]{2,1,0:T(1,128)}), f32[128,1,1]{2,1,0:T(1,128)S(1)}, u32[]{:S(2)}, u32[]{:S(2)}) async-start(f32[128,1,1]{2,1,0:T(1,128)} %copy.46), calls=%async_computation | async-start | bytes 131072 | tf_op jit(solution)/shard_map/all_to_all | solution.py:68
  22.3 6.5 %gather_fusion.1 = f32[128,128,128]{2,1,0:T(8,128)} fusion(f32[64,128,128]{2,1,0:T(8,128)} %param.15, s32[1024]{0:T(1024)S(1)} %pad_clamp_fusion), kind=kCustom, calls=%fused_computation.1 | custom fusion | bytes 16777728 | tf_op jit(solution)/shard_map/jit(_take)/gather | solution.py:63
  28.8 6.4 %select_select_fusion = f32[128,128,128]{2,1,0:T(8,128)} fusion(f32[128,128,128]{2,1,0:T(8,128)} %gather_fusion.1, pred[128]{0:T(512)(128)(4,1)S(1)} %compare_and_fusion, pred[128]{0:T(512)(128)(4,1)S(1)} %fusion.27), kind=kLoop, calls=%fused_computation.4 | loop fusion | flops 4194304 | bytes 16777472 | tf_op jit(solution)/shard_map/jit(_where)/select_n | solution.py:64
  35.2 10.2 %all-to-all-start.1 = ((f32[128,128,128]{2,1,0:T(8,128)}), f32[128,128,128]{2,1,0:T(8,128)}, u32[]{:S(2)}, u32[]{:S(2)}) async-start(f32[128,128,128]{2,1,0:T(8,128)} %select_select_fusion), calls=%async_computation.1 | async-start | bytes 16777216 | tf_op jit(solution)/shard_map/all_to_all | solution.py:67
  45.7 1.0 reduce.8
  46.7 104.0 %all-to-all-done.1 = f32[128,128,128]{2,1,0:T(8,128)} async-done(((f32[128,128,128]{2,1,0:T(8,128)}), f32[128,128,128]{2,1,0:T(8,128)}, u32[]{:S(2)}, u32[]{:S(2)}) %all-to-all-start.1) | async-done | bytes 8388640 | tf_op jit(solution)/shard_map/all_to_all | solution.py:67
  150.8 9.3 %copy.58 = f32[128,128,128]{0,2,1:T(8,128)} copy(f32[128,128,128]{2,1,0:T(8,128)} %all-to-all-done.1) | data formatting | bytes 16777216 | tf_op jit(solution)/shard_map/reshape | solution.py:74
  160.1 12.3 %bitcast_add_fusion = f32[3,24,128,128]{3,1,2,0:T(8,128)S(1)} fusion(f32[3,1,24,1,128,128]{5,4,3,2,1,0:T(8,128)} %param.14, f32[128,128,128]{0,2,1:T(8,128)} %copy.58, f32[3,24]{1,0:T(4,128)S(1)} %multiply_add_fusion, f32[128]{0:T(128)S(1)} %reduce.8), kind=kOutput, calls=%fused_computation.9 | convolution fusion | flops 1813128192 | bytes 17826592 | tf_op jit(solution)/shard_map/dot_general | solution.py:73
  172.4 2.2 copy-done.3
  175.7 0.8 broadcast_select_fusion.1
  176.6 37.1 %all-reduce.3.cloned.1.call-done = f32[3,128,256]{2,1,0:T(8,128)} async-done(((f32[3,128,256]{2,1,0:T(8,128)}), f32[3,128,256]{2,1,0:T(8,128)}) %all-reduce.3.cloned.1.call-update) | async-done | bytes 393232 | tf_op jit(solution)/shard_map/psum | solution.py:27
  214.1 68.0 %all-gather.5.cloned.1.call-done = f32[3,4096,256]{2,1,0:T(8,128)} async-done(((f32[3,128,256]{2,1,0:T(8,128)}), f32[3,4096,256]{2,1,0:T(8,128)}) %all-gather.5.cloned.1.call-update) | async-done | bytes 12582928 | tf_op jit(solution)/shard_map/all_gather | solution.py:33
  282.1 6.4 %fusion.6 = f32[24,128,3,128]{1,3,2,0:T(8,128)S(1)} fusion(f32[24,4,128,256]{3,2,1,0:T(8,128)} %bitcast.106, s32[]{:T(128)S(6)} %select_n.140, f32[3,128,256]{2,1,0:T(8,128)} %all-reduce.3.cloned.1.call-done), kind=kOutput, calls=%fused_computation.12 | convolution fusion | flops 3623878656 | bytes 8257540 | tf_op jit(solution)/shard_map/aik,bjk->abij/dot_general | solution.py:45
  288.6 3.2 fusion.3
  291.8 2.2 copy-done.4
  294.5 0.5 fusion.13
  295.0 0.8 broadcast_select_fusion
  296.2 39.0 %all-reduce.5.cloned.1.call-done = f32[3,128,256]{2,1,0:T(8,128)} async-done(((f32[3,128,256]{2,1,0:T(8,128)}), f32[3,128,256]{2,1,0:T(8,128)}) %all-reduce.5.cloned.1.call-update) | async-done | bytes 393232 | tf_op jit(solution)/shard_map/psum | solution.py:27
  335.3 68.1 %all-gather.7.cloned.1.call-done = f32[3,4096,256]{2,1,0:T(8,128)} async-done(((f32[3,128,256]{2,1,0:T(8,128)}), f32[3,4096,256]{2,1,0:T(8,128)}) %all-gather.7.cloned.1.call-update) | async-done | bytes 12582928 | tf_op jit(solution)/shard_map/all_gather | solution.py:33
  403.5 8.3 %fusion.4 = f32[24,128,3,128]{3,1,2,0:T(8,128)} fusion(f32[24,4,128,256]{3,2,1,0:T(8,128)} %bitcast.107, s32[]{:T(128)S(6)} %select_n.140, f32[3,128,256]{2,1,0:T(8,128)} %all-reduce.5.cloned.1.call-done), kind=kOutput, calls=%fused_computation.10 | convolution fusion | flops 3623878656 | bytes 8257540 | tf_op jit(solution)/shard_map/aik,bjk->abij/dot_general | solution.py:45
  411.8 6.1 %copy.49 = f32[24,128,3,128]{1,0,3,2:T(8,128)} copy(f32[24,128,3,128]{3,1,2,0:T(8,128)} %fusion.4) | data formatting | bytes 9437184 | tf_op jit(solution)/shard_map/aik,bjk->abij/dot_general | solution.py:45
  417.8 4.4 fusion.2
  422.2 2.1 copy-done.2
  424.5 6.5 %scatter.14 = f32[3,1,24,1,128,128]{5,2,4,0,3,1:T(8,128)} dynamic-update-slice(f32[3,1,24,1,128,128]{5,2,4,0,3,1:T(8,128)} %bitcast.97, f32[3,1,1,1,128,128]{5,2,4,0,3,1:T(1,128)S(1)} %bitcast.111, s32[]{:T(128)} %constant.145.clone.1, s32[]{:T(128)} %constant.145.clone.1, s32[]{:T(128)} %constant.145.clone.1, s32[]{:T(128)} %constant.145.clone.1, s32[]{:T(128)} %constant.145.clone.1, ...) | dynamic-update-slice | bytes 393220 | tf_op jit(solution)/shard_map/scatter | solution.py:89
  431.0 6.5 %scatter.15 = f32[3,1,24,1,128,128]{5,2,4,0,3,1:T(8,128)} dynamic-update-slice(f32[3,1,24,1,128,128]{5,2,4,0,3,1:T(8,128)} %scatter.14, f32[3,1,1,1,128,128]{5,2,4,0,3,1:T(1,128)S(1)} %bitcast.110, s32[]{:T(128)} %constant.145.clone.1, s32[]{:T(128)} %constant.145.clone.1, s32[]{:T(128)} %constant.145.clone.1, s32[]{:T(128)} %constant.145.clone.1, s32[]{:T(128)} %constant.145.clone.1, ...) | dynamic-update-slice | bytes 393220 | tf_op jit(solution)/shard_map/scatter | solution.py:89
  437.5 6.5 %scatter.16 = f32[3,1,24,1,128,128]{5,2,4,0,3,1:T(8,128)} dynamic-update-slice(f32[3,1,24,1,128,128]{5,2,4,0,3,1:T(8,128)} %scatter.15, f32[3,1,1,1,128,128]{5,2,4,0,3,1:T(1,128)S(1)} %bitcast.109, s32[]{:T(128)} %constant.145.clone.1, s32[]{:T(128)} %constant.145.clone.1, s32[]{:T(128)} %constant.145.clone.1, s32[]{:T(128)} %constant.145.clone.1, s32[]{:T(128)} %constant.145.clone.1, ...) | dynamic-update-slice | bytes 393220 | tf_op jit(solution)/shard_map/scatter | solution.py:89
  444.0 6.5 %scatter.19 = f32[3,1,24,1,128,128]{5,2,4,0,3,1:T(8,128)} dynamic-update-slice(f32[3,1,24,1,128,128]{5,2,4,0,3,1:T(8,128)} %scatter.16, f32[3,1,1,1,128,128]{5,2,4,0,3,1:T(1,128)S(1)} %bitcast.108, s32[]{:T(128)} %constant.145.clone.1, s32[]{:T(128)} %constant.145.clone.1, s32[]{:T(128)} %constant.145.clone.1, s32[]{:T(128)} %constant.145.clone.1, s32[]{:T(128)} %constant.145.clone.1, ...) | dynamic-update-slice | bytes 393220 | tf_op jit(solution)/shard_map/scatter | solution.py:89
  450.5 5.3 %copy.54 = f32[3,1,24,1,128,128]{5,4,3,2,1,0:T(8,128)} copy(f32[3,1,24,1,128,128]{5,2,4,0,3,1:T(8,128)} %scatter.19) | data formatting | bytes 9437184 | tf_op jit(solution)/shard_map/scatter | solution.py:89
  (47 shorter events, 2.9 us)
Async XLA Ops:
  6.5 2.2 copy-start
  10.8 24.5 %all-to-all-start = ((f32[128,1,1]{2,1,0:T(1,128)}), f32[128,1,1]{2,1,0:T(1,128)S(1)}, u32[]{:S(2)}, u32[]{:S(2)}) async-start(f32[128,1,1]{2,1,0:T(1,128)} %copy.46), calls=%async_computation | async-start | bytes 131072 | tf_op jit(solution)/shard_map/all_to_all | solution.py:68
  35.2 115.6 %all-to-all-start.1 = ((f32[128,128,128]{2,1,0:T(8,128)}), f32[128,128,128]{2,1,0:T(8,128)}, u32[]{:S(2)}, u32[]{:S(2)}) async-start(f32[128,128,128]{2,1,0:T(8,128)} %select_select_fusion), calls=%async_computation.1 | async-start | bytes 16777216 | tf_op jit(solution)/shard_map/all_to_all | solution.py:67
  45.4 168.2 %all-reduce.3.cloned.1.call-start = ((), (), s32[]{:S(2)}) async-start(), calls=%async_computation.2 | async-start | bytes 786432 | tf_op jit(solution)/shard_map/psum | solution.py:27
  160.1 14.6 %copy-start.7 = (f32[2,256,256]{2,1,0:T(8,128)S(1)}, f32[2,256,256]{2,1,0:T(8,128)}, u32[]{:S(2)}) copy-start(f32[2,256,256]{2,1,0:T(8,128)} %param.19) | copy-start | bytes 1572868
  172.4 2.2 copy-start.3
  176.5 112.0 %slice-start = ((s8[4718592]{0:T(1024)(128)(4,1)}), s8[524288]{0:T(1024)(128)(4,1)S(1)}, s32[]{:S(2)}) async-start(s8[4718592]{0:T(1024)(128)(4,1)} %bitcast.98), calls=%async_computation.6 | async-start | bytes 1048576
  176.5 105.5 %all-gather.5.cloned.1.call-start = ((), (), s32[]{:S(2)}) async-start(), calls=%async_computation.4 | async-start | bytes 12976128 | tf_op jit(solution)/shard_map/all_gather | solution.py:33
  213.7 121.5 %all-reduce.5.cloned.1.call-start = ((), (), s32[]{:S(2)}) async-start(), calls=%async_computation.3 | async-start | bytes 786432 | tf_op jit(solution)/shard_map/psum | solution.py:27
  282.1 6.5 %slice-start.1 = ((s8[4718592]{0:T(1024)(128)(4,1)}), s8[4194304]{0:T(1024)(128)(4,1)S(1)}, s32[]{:S(2)}) async-start(s8[4718592]{0:T(1024)(128)(4,1)} %bitcast.98), calls=%async_computation.7 | async-start | bytes 8388608
  291.8 2.2 copy-start.4
  295.9 107.6 %all-gather.7.cloned.1.call-start = ((), (), s32[]{:S(2)}) async-start(), calls=%async_computation.5 | async-start | bytes 12976128 | tf_op jit(solution)/shard_map/all_gather | solution.py:33
  417.8 6.6 %copy-start.5 = (f32[3,128,256]{2,1,0:T(8,128)S(1)}, f32[3,128,256]{2,1,0:T(8,128)}, u32[]{:S(2)}) copy-start(f32[3,128,256]{2,1,0:T(8,128)} %all-reduce.3.cloned.1.call-done) | copy-start | bytes 1179652
  417.8 6.6 %copy-start.6 = (f32[3,128,256]{2,1,0:T(8,128)S(1)}, f32[3,128,256]{2,1,0:T(8,128)}, u32[]{:S(2)}) copy-start(f32[3,128,256]{2,1,0:T(8,128)} %all-reduce.5.cloned.1.call-done) | copy-start | bytes 1179652
  422.2 2.1 copy-start.2
  444.0 11.8 %copy-start.1 = (s32[64]{0:T(128)S(1)}, s32[64]{0:T(128)}, u32[]{:S(2)}) copy-start(s32[64]{0:T(128)} %param.17) | copy-start | bytes 772
Sparse Core Ops, SparseCore 0:
  176.7 36.9 all-reduce.2
  216.0 66.0 all-gather.4
  296.0 39.1 all-reduce.4
  337.4 66.0 all-gather.6
where the time goes:
time: 463 us; the launch traced here: 462 us
  waiting for transfers between devices  316 us (68%)
  local copies, waits for them, and re-layouts  61.9 us (13%)
  matrix products  28.9 us (6%)
  starting transfers between devices  22.5 us (5%)
  other arithmetic  18.5 us (4%)
  between operations  14.1 us (3%)
    all_gather x2, waiting for transfers between devices, column_side(): lax.all_gather(rows_three.reshape(rows_here, 1, tile, 2 * tile), 'row', a...  136 us
    all_to_all x1, waiting for transfers between devices, body(): lax.all_to_all(outgoing, ('row', 'col'), split_axis=0, concat_axis=0, til...  104 us
    psum x2, waiting for transfers between devices, panel_rows(): summed = lax.psum(total, 'col')  76.1 us
    scatter x5, local copies, waits for them, and re-layouts, body(): field.at[:, local_b]  31.3 us
    dot_general x2, matrix products, trailing(): jnp.einsum('aik,bjk->abij', rows_three, cols_three, precision=lax.Precisi...  14.7 us
    dot_general x1, matrix products, body(): jnp.dot(placing, incoming.reshape(devices, tile * tile), precision=lax.Pr...  12.3 us
    all_to_all x1, starting transfers between devices, body(): lax.all_to_all(slot_out, ('row', 'col'), split_axis=0, concat_axis=0, til...  11.5 us
    all_to_all x1, starting transfers between devices, body(): lax.all_to_all(outgoing, ('row', 'col'), split_axis=0, concat_axis=0, til...  10.2 us
  transfers between devices with their start and end apart: 6, of which 5 were waited for; matrix products, arithmetic and copies ran while one was open for 3% of the time, Pallas kernels for 0%

commit v1 on v0

--- a/solution.py
+++ b/solution.py
@@ -30,8 +30,14 @@
 
 def column_side(rows_three, cols_here, my_col, n_col):
     rows_here, tile = (rows_three.shape[0], rows_three.shape[1])
-    whole = lax.all_gather(
-        rows_three.reshape(rows_here, 1, tile, 2 * tile), "row", axis=1, tiled=True
+    whole = jnp.concatenate(
+        lax.all_to_all(
+            jnp.stack([rows_three.reshape(rows_here, 1, tile, 2 * tile)] * lax.axis_size("row")),
+            "row",
+            0,
+            0,
+        ),
+        axis=1,
     )
     ordered = whole.reshape(cols_here, n_col, tile, 2 * tile)
     return lax.dynamic_index_in_dim(ordered, my_col, axis=1, keepdims=False)

time: 463 us -> 778 us (1.68)
  the two profiles are of different devices: /device:TPU:1 before, /device:TPU:36 now
where the time goes in v1:
time: 778 us; the launch traced here: 777 us
  waiting for transfers between devices  579 us (74%)
  local copies, waits for them, and re-layouts  97.4 us (13%)
  starting transfers between devices  35.9 us (5%)
  matrix products  28.7 us (4%)
  other arithmetic  20.8 us (3%)
  between operations  14.3 us (2%)
    all_to_all x2, waiting for transfers between devices, column_side(): lax.all_to_all(jnp.stack([rows_three.reshape(rows_here, 1, tile, 2 * tile...  395 us
    all_to_all x1, waiting for transfers between devices, body(): lax.all_to_all(outgoing, ('row', 'col'), split_axis=0, concat_axis=0, til...  98.6 us
    psum x2, waiting for transfers between devices, panel_rows(): summed = lax.psum(total, 'col')  86.1 us
    scatter x5, local copies, waits for them, and re-layouts, body(): field.at[:, local_b]  31.3 us
    all_to_all x2, local copies, waits for them, and re-layouts, column_side(): lax.all_to_all(jnp.stack([rows_three.reshape(rows_here, 1, tile, 2 * tile...  21.3 us
  transfers between devices with their start and end apart: 6, of which 5 were waited for; matrix products, arithmetic and copies ran while one was open for 2% of the time, Pallas kernels for 0%

profile of v1, /device:TPU:36, one launch (start us, length us, event | category | flops | bytes accessed | tf_op | source)
XLA Modules:
  0.0 776.6 jit_solution(9012710962859182783)
XLA Ops:
  8.8 1.2 gather_fusion
  10.8 10.2 %all-to-all-start = ((f32[128,1,1]{2,1,0:T(1,128)}), f32[128,1,1]{2,1,0:T(1,128)S(1)}, u32[]{:S(2)}, u32[]{:S(2)}) async-start(f32[128,1,1]{2,1,0:T(1,128)} %copy.50), calls=%async_computation | async-start | bytes 131072 | tf_op jit(solution)/shard_map/all_to_all | solution.py:74
  21.0 6.5 gather_fusion.1
  27.5 6.4 select_select_fusion
  33.9 10.2 %all-to-all-start.1 = ((f32[128,128,128]{2,1,0:T(8,128)}), f32[128,128,128]{2,1,0:T(8,128)}, u32[]{:S(2)}, u32[]{:S(2)}) async-start(f32[128,128,128]{2,1,0:T(8,128)} %select_select_fusion), calls=%async_computation.1 | async-start | bytes 16777216 | tf_op jit(solution)/shard_map/all_to_all | solution.py:73
  44.4 1.0 reduce.8
  45.4 98.6 %all-to-all-done.1 = f32[128,128,128]{2,1,0:T(8,128)} async-done(((f32[128,128,128]{2,1,0:T(8,128)}), f32[128,128,128]{2,1,0:T(8,128)}, u32[]{:S(2)}, u32[]{:S(2)}) %all-to-all-start.1) | async-done | bytes 8388640 | tf_op jit(solution)/shard_map/all_to_all | solution.py:73
  144.0 9.3 %copy.64 = f32[128,128,128]{0,2,1:T(8,128)} copy(f32[128,128,128]{2,1,0:T(8,128)} %all-to-all-done.1) | data formatting | bytes 16777216 | tf_op jit(solution)/shard_map/reshape | solution.py:80
  153.3 12.3 %bitcast_add_fusion = f32[3,24,128,128]{3,1,2,0:T(8,128)S(1)} fusion(f32[3,1,24,1,128,128]{5,4,3,2,1,0:T(8,128)} %param.14, f32[128,128,128]{0,2,1:T(8,128)} %copy.64, f32[3,24]{1,0:T(4,128)S(1)} %multiply_add_fusion, f32[128]{0:T(128)S(1)} %reduce.8), kind=kOutput, calls=%fused_computation.9 | convolution fusion | flops 1813128192 | bytes 17826592 | tf_op jit(solution)/shard_map/dot_general | solution.py:79
  165.7 2.2 copy-done.3
  169.8 44.8 %all-reduce.3.cloned.1.call-done = f32[3,128,256]{2,1,0:T(8,128)} async-done(((f32[3,128,256]{2,1,0:T(8,128)}), f32[3,128,256]{2,1,0:T(8,128)}) %all-reduce.3.cloned.1.call-update) | async-done | bytes 393232 | tf_op jit(solution)/shard_map/psum | solution.py:27
  214.6 7.0 stack.6
  221.6 7.5 all-to-all-start.2
  229.5 196.5 %all-to-all-done.2 = f32[32,3,1,128,256]{4,3,1,2,0:T(8,128)} async-done(((f32[32,3,1,128,256]{4,3,1,2,0:T(8,128)}), f32[32,3,1,128,256]{4,3,1,2,0:T(8,128)}, u32[]{:S(2)}, u32[]{:S(2)}) %all-to-all-start.2) | async-done | bytes 12582944 | tf_op jit(solution)/shard_map/all_to_all | solution.py:34
  426.0 10.6 %copy.52 = f32[32,3,1,128,256]{4,3,0,1,2:T(8,128)} copy(f32[32,3,1,128,256]{4,3,1,2,0:T(8,128)} %all-to-all-done.2) | data formatting | bytes 25165824 | tf_op jit(solution)/shard_map/all_to_all | solution.py:34
  436.7 6.3 fusion.6
  442.9 5.5 fusion.3
  448.5 2.2 copy-done.4
  452.6 41.3 %all-reduce.5.cloned.1.call-done = f32[3,128,256]{2,1,0:T(8,128)} async-done(((f32[3,128,256]{2,1,0:T(8,128)}), f32[3,128,256]{2,1,0:T(8,128)}) %all-reduce.5.cloned.1.call-update) | async-done | bytes 393232 | tf_op jit(solution)/shard_map/psum | solution.py:27
  493.9 7.1 stack.7
  501.0 7.5 all-to-all-start.3
  508.6 198.3 %all-to-all-done.3 = f32[32,3,1,128,256]{4,3,1,2,0:T(8,128)} async-done(((f32[32,3,1,128,256]{4,3,1,2,0:T(8,128)}), f32[32,3,1,128,256]{4,3,1,2,0:T(8,128)}, u32[]{:S(2)}, u32[]{:S(2)}) %all-to-all-start.3) | async-done | bytes 12582944 | tf_op jit(solution)/shard_map/all_to_all | solution.py:34
  706.9 10.7 %copy.54 = f32[32,3,1,128,256]{4,3,0,1,2:T(8,128)} copy(f32[32,3,1,128,256]{4,3,1,2,0:T(8,128)} %all-to-all-done.3) | data formatting | bytes 25165824 | tf_op jit(solution)/shard_map/all_to_all | solution.py:34
  717.6 8.2 %fusion.4 = f32[24,128,3,128]{3,1,2,0:T(8,128)} fusion(f32[24,4,128,256]{3,2,1,0:T(8,128)} %bitcast.102, s32[]{:T(128)S(6)} %select_n.140, f32[3,128,256]{2,1,0:T(8,128)S(1)} %copy-done.6), kind=kOutput, calls=%fused_computation.10 | convolution fusion | flops 3623878656 | bytes 8257540 | tf_op jit(solution)/shard_map/aik,bjk->abij/dot_general | solution.py:51
  725.8 6.1 copy.55
  731.9 4.3 fusion.2
  736.2 2.1 copy-done.2
  738.5 6.5 scatter.14
  745.0 6.5 scatter.15
  751.5 6.5 scatter.16
  758.0 6.5 scatter.19
  764.5 5.3 copy.60
  (44 shorter events, 7.0 us)
Async XLA Ops:
  6.5 2.2 copy-start
  10.8 23.2 %all-to-all-start = ((f32[128,1,1]{2,1,0:T(1,128)}), f32[128,1,1]{2,1,0:T(1,128)S(1)}, u32[]{:S(2)}, u32[]{:S(2)}) async-start(f32[128,1,1]{2,1,0:T(1,128)} %copy.50), calls=%async_computation | async-start | bytes 131072 | tf_op jit(solution)/shard_map/all_to_all | solution.py:74
  33.9 110.1 %all-to-all-start.1 = ((f32[128,128,128]{2,1,0:T(8,128)}), f32[128,128,128]{2,1,0:T(8,128)}, u32[]{:S(2)}, u32[]{:S(2)}) async-start(f32[128,128,128]{2,1,0:T(8,128)} %select_select_fusion), calls=%async_computation.1 | async-start | bytes 16777216 | tf_op jit(solution)/shard_map/all_to_all | solution.py:73
  44.1 170.5 %all-reduce.3.cloned.1.call-start = ((), (), s32[]{:S(2)}) async-start(), calls=%async_computation.4 | async-start | bytes 786432 | tf_op jit(solution)/shard_map/psum | solution.py:27
  153.3 14.6 %copy-start.7 = (f32[2,256,256]{2,1,0:T(8,128)S(1)}, f32[2,256,256]{2,1,0:T(8,128)}, u32[]{:S(2)}) copy-start(f32[2,256,256]{2,1,0:T(8,128)} %param.19) | copy-start | bytes 1572868
  165.7 2.2 copy-start.3
  221.6 204.4 %all-to-all-start.2 = ((f32[32,3,1,128,256]{4,3,1,2,0:T(8,128)}), f32[32,3,1,128,256]{4,3,1,2,0:T(8,128)}, u32[]{:S(2)}, u32[]{:S(2)}) async-start(f32[32,3,1,128,256]{4,3,1,2,0:T(8,128)} %stack.6), calls=%async_computation.2 | async-start | bytes 25165824 | tf_op jit(solution)/shard_map/all_to_all | solution.py:34
  229.2 264.8 %all-reduce.5.cloned.1.call-start = ((), (), s32[]{:S(2)}) async-start(), calls=%async_computation.5 | async-start | bytes 786432 | tf_op jit(solution)/shard_map/psum | solution.py:27
  229.5 207.1 %copy-start.5 = (f32[3,128,256]{2,1,0:T(8,128)S(1)}, f32[3,128,256]{2,1,0:T(8,128)}, u32[]{:S(2)}) copy-start(f32[3,128,256]{2,1,0:T(8,128)} %all-reduce.3.cloned.1.call-done) | copy-start | bytes 1179652
  448.5 2.2 copy-start.4
  501.0 205.9 %all-to-all-start.3 = ((f32[32,3,1,128,256]{4,3,1,2,0:T(8,128)}), f32[32,3,1,128,256]{4,3,1,2,0:T(8,128)}, u32[]{:S(2)}, u32[]{:S(2)}) async-start(f32[32,3,1,128,256]{4,3,1,2,0:T(8,128)} %stack.7), calls=%async_computation.3 | async-start | bytes 25165824 | tf_op jit(solution)/shard_map/all_to_all | solution.py:34
  508.6 209.0 %copy-start.6 = (f32[3,128,256]{2,1,0:T(8,128)S(1)}, f32[3,128,256]{2,1,0:T(8,128)}, u32[]{:S(2)}) copy-start(f32[3,128,256]{2,1,0:T(8,128)} %all-reduce.5.cloned.1.call-done) | copy-start | bytes 1179652
  736.2 2.1 copy-start.2
  758.0 11.8 %copy-start.1 = (s32[64]{0:T(128)S(1)}, s32[64]{0:T(128)}, u32[]{:S(2)}) copy-start(s32[64]{0:T(128)} %param.17) | copy-start | bytes 772
Sparse Core Ops, SparseCore 0:
  169.9 44.6 all-reduce.2
  452.7 41.1 all-reduce.4
